TPU v7x, 512 devices: a whole 4x8x8 slice. The times are simulated.
512 devices in a mesh: dp: 16 (over z, core), tp: 4 (over y_lo), cp: 8 (over y_hi, x).
Axes of the slice: x: 4, y: 8 (y_hi: 2, y_lo: 4; y = y_hi * 4 + y_lo), z: 8, core: 2. Of those that a mesh axis runs over, the one named last changes fastest.
Arguments:
- tokens: bfloat16 [65536, 1024], P(('dp', 'tp', 'cp')), may hold values from -6 to 6
- expert_ids: int32 [65536, 2], P(('dp', 'tp', 'cp')), may hold values from 0 to 31, all different within a row; in each aligned block of 128 rows (0 to 127, 128 to 255, ...) at most 12 rows name the same one
- router_weight: bfloat16 [1024, 32], replicated, may hold values from -0.1875 to 0.1875
- gate_weight: bfloat16 [32, 1024, 384], P(('tp', 'cp'), 'dp'), may hold values from -0.1875 to 0.1875
- up_weight: bfloat16 [32, 1024, 384], P(('tp', 'cp'), 'dp'), may hold values from -0.1875 to 0.1875
- down_weight: bfloat16 [32, 384, 1024], P(('tp', 'cp'), None, 'dp'), may hold values from -0.3125 to 0.3125
- grad_out: bfloat16 [65536, 1024], P(('dp', 'tp', 'cp')), may hold values from -6 to 6
Outputs:
- moe_out: bfloat16 [65536, 1024], P(('dp', 'tp', 'cp'))
- grad_tokens: bfloat16 [65536, 1024], P(('dp', 'tp', 'cp'))
- router_grad: float32 [1024, 32], replicated
Inputs may be any that keep to these rules, and one draw needn't show every extreme that they name: `expert_ids`: each row names 2 different experts. Among the 128 rows of one device no expert is named by more than 12 rows, a bound that some block reaches.
All inputs are finite; a program needn't handle non-finite values.
Results may differ from a plain program's by a relative error of at most 0.0064.
Values may be sent and summed in bfloat16 or wider, within the bound.
A program may use at most 64 MiB of HBM per device.

v0:
```python
import jax
import jax.numpy as jnp
from jax import lax
from jax.sharding import PartitionSpec as P


def route_slots(flat_ids, expert_count):
    hits = (flat_ids[:, None] == jnp.arange(expert_count, dtype=jnp.int32)[None, :]).astype(
        jnp.int32
    )
    before = jnp.cumsum(hits, axis=0) - hits
    return jnp.sum(before * hits, axis=1)


def trade(stacked, capacity):
    item_count = stacked.shape[0]
    feature_dim = stacked.shape[2]
    tp_count = lax.axis_size("tp")
    cp_count = lax.axis_size("cp")
    shaped = stacked.reshape(item_count, tp_count * cp_count, capacity, feature_dim)
    moved = lax.all_to_all(shaped, ("tp", "cp"), split_axis=1, concat_axis=1, tiled=True)
    return moved.reshape(item_count, -1, feature_dim)


def expert_forward(received, w_gate, w_up, w_down):
    gate_act = jnp.dot(received, w_gate, preferred_element_type=jnp.float32)
    up_act = jnp.dot(received, w_up, preferred_element_type=jnp.float32)
    hidden = (jax.nn.silu(gate_act) * up_act).astype(jnp.bfloat16)
    produced = jnp.dot(hidden, w_down, preferred_element_type=jnp.float32).astype(jnp.bfloat16)
    return (gate_act, up_act, produced)


def expert_backward(received_grad, gate_act, up_act, w_gate, w_up, w_down):
    contract = (((1,), (1,)), ((), ()))
    grad_hidden = lax.dot_general(
        received_grad, w_down, contract, preferred_element_type=jnp.float32
    )
    sigma = jax.nn.sigmoid(gate_act)
    grad_gate = (grad_hidden * up_act * sigma * (1.0 + gate_act * (1.0 - sigma))).astype(
        jnp.bfloat16
    )
    grad_up = (grad_hidden * gate_act * sigma).astype(jnp.bfloat16)
    returned = lax.dot_general(grad_gate, w_gate, contract, preferred_element_type=jnp.float32)
    returned = returned + lax.dot_general(
        grad_up, w_up, contract, preferred_element_type=jnp.float32
    )
    return returned.astype(jnp.bfloat16)


def on_device(tokens, expert_ids, router_weight, gate_weight, up_weight, down_weight, grad_out):
    row_count, feature_dim = tokens.shape
    topk = expert_ids.shape[1]
    groups = lax.axis_size(("tp", "cp"))
    capacity = 3 * row_count * topk // (2 * groups)
    expert_count = router_weight.shape[1]
    contract = (((1,), (1,)), ((), ()))
    w_gate, w_up, w_down = (
        lax.all_gather(gate_weight[0], "dp", axis=0, tiled=True),
        lax.all_gather(up_weight[0], "dp", axis=0, tiled=True),
        lax.all_gather(down_weight[0], "dp", axis=1, tiled=True),
    )
    logits = jnp.dot(tokens, router_weight, preferred_element_type=jnp.float32)
    chosen = jnp.take_along_axis(logits, expert_ids, axis=1)
    mixing = 1.0 / jnp.sum(jnp.exp(chosen[:, None, :] - chosen[:, :, None]), axis=2)
    flat_ids = expert_ids.reshape(-1)
    slots = route_slots(flat_ids, expert_count)
    position = flat_ids * capacity + slots
    slot_total = groups * capacity
    repeated = jnp.repeat(tokens, topk, axis=0)
    scaled_grad = (mixing[:, :, None] * grad_out.astype(jnp.float32)[:, None, :]).astype(
        jnp.bfloat16
    )
    scaled_flat = scaled_grad.reshape(-1, feature_dim)
    sent = jnp.zeros((1, slot_total, feature_dim), jnp.bfloat16).at[0, position].set(repeated)
    received = trade(sent, capacity)[0]
    gate_act, up_act, produced = expert_forward(received, w_gate, w_up, w_down)
    came_back = trade(produced[None], capacity)[0]
    sent_grad = (
        jnp.zeros((1, slot_total, feature_dim), jnp.bfloat16).at[0, position].set(scaled_flat)
    )
    received_grad = trade(sent_grad, capacity)[0]
    returned = expert_backward(received_grad, gate_act, up_act, w_gate, w_up, w_down)
    back_home = trade(returned[None], capacity)[0]
    out_rows = jnp.take(came_back, position, axis=0).reshape(row_count, topk, feature_dim)
    moe_out = jnp.sum(mixing[:, :, None] * out_rows.astype(jnp.float32), axis=1).astype(
        jnp.bfloat16
    )
    back_rows = jnp.take(back_home, position, axis=0).reshape(row_count, topk, feature_dim)
    scores = jnp.einsum("td,tkd->tk", grad_out, out_rows, preferred_element_type=jnp.float32)
    dlogit = mixing * (scores - jnp.sum(mixing * scores, axis=1, keepdims=True))
    onehot = (
        expert_ids[:, :, None] == jnp.arange(expert_count, dtype=jnp.int32)[None, None, :]
    ).astype(jnp.float32)
    dense = jnp.sum(onehot * dlogit[:, :, None], axis=1).astype(jnp.bfloat16)
    router_back = lax.dot_general(
        dense, router_weight, contract, preferred_element_type=jnp.float32
    )
    grad_tokens = (jnp.sum(back_rows.astype(jnp.float32), axis=1) + router_back).astype(
        jnp.bfloat16
    )
    router_part = lax.dot_general(
        tokens, dense, (((0,), (0,)), ((), ())), preferred_element_type=jnp.float32
    )
    router_grad = lax.psum(router_part, ("dp", "tp", "cp"))
    return (moe_out, grad_tokens, router_grad)


def solution(mesh):
    in_specs = (
        P(("dp", "tp", "cp"), None),
        P(("dp", "tp", "cp"), None),
        P(),
        P(("tp", "cp"), "dp", None),
        P(("tp", "cp"), "dp", None),
        P(("tp", "cp"), None, "dp"),
        P(("dp", "tp", "cp"), None),
    )
    out_specs = (P(("dp", "tp", "cp"), None), P(("dp", "tp", "cp"), None), P())
    return jax.shard_map(
        on_device, mesh=mesh, in_specs=in_specs, out_specs=out_specs, check_vma=False
    )
```

profile of v0, /device:TPU:1, one launch (start us, length us, event | category | flops | bytes accessed | tf_op | source)
XLA Modules:
  0.0 453.8 jit_solution(12045069232960749352)
XLA Ops:
  10.1 1.2 broadcast_in_dim.16
  11.6 1.9 scatter_custom_fusion
  13.5 1.2 reshape.105
  14.7 10.6 %all-to-all-start = ((bf16[1,32,12,1024]{3,2,0,1:T(8,128)(2,1)}), bf16[1,32,12,1024]{3,2,0,1:T(8,128)(2,1)S(1)}, u32[]{:S(2)}, u32[]{:S(2)}) async-start(bf16[1,32,12,1024]{3,2,0,1:T(8,128)(2,1)} %bitcast.4), calls=%async_computation | async-start | bytes 2097152 | tf_op jit(solution)/shard_map/all_to_all | solution.py:21
  25.3 27.5 %all-gather.2 = bf16[1,384,1024]{1,2,0:T(8,128)(2,1)} all-gather(bf16[1,384,64]{1,2,0:T(8,128)(2,1)S(1)} %copy-done.15), channel_id=4, replica_groups=mesh['dp'=16,'tp'=4,'cp'=8] {'dp'}, dimensions={2}, use_global_device_ids=true | all-gather | bytes 835584 | tf_op jit(solution)/shard_map/all_gather | solution.py:60
  52.9 16.6 %all-gather.1 = bf16[1,1024,384]{2,1,0:T(8,128)(2,1)S(1)} all-gather(bf16[1,64,384]{2,1,0:T(8,128)(2,1)S(1)} %copy-done.16), channel_id=3, replica_groups=mesh['dp'=16,'tp'=4,'cp'=8] {'dp'}, dimensions={1}, use_global_device_ids=true | all-gather | bytes 835584 | tf_op jit(solution)/shard_map/all_gather | solution.py:59
  69.5 17.9 %all-gather = bf16[1,1024,384]{2,1,0:T(8,128)(2,1)S(1)} all-gather(bf16[1,64,384]{2,1,0:T(8,128)(2,1)S(1)} %copy-done.17), channel_id=2, replica_groups=mesh['dp'=16,'tp'=4,'cp'=8] {'dp'}, dimensions={1}, use_global_device_ids=true | all-gather | bytes 835584 | tf_op jit(solution)/shard_map/all_gather | solution.py:58
  90.5 1.2 reshape_broadcast_in_dim.6
  91.8 9.6 %all-to-all-start.1 = ((bf16[1,32,12,1024]{3,2,0,1:T(8,128)(2,1)}), bf16[1,32,12,1024]{3,2,0,1:T(8,128)(2,1)S(1)}, u32[]{:S(2)}, u32[]{:S(2)}) async-start(bf16[1,32,12,1024]{3,2,0,1:T(8,128)(2,1)} %bitcast.8), calls=%async_computation.1 | async-start | bytes 2097152 | tf_op jit(solution)/shard_map/all_to_all | solution.py:21
  101.9 2.0 gather_fusion
  104.4 1.7 mul.98
  106.1 21.9 %all-to-all-done.1 = bf16[1,32,12,1024]{3,2,0,1:T(8,128)(2,1)S(1)} async-done(((bf16[1,32,12,1024]{3,2,0,1:T(8,128)(2,1)}), bf16[1,32,12,1024]{3,2,0,1:T(8,128)(2,1)S(1)}, u32[]{:S(2)}, u32[]{:S(2)}) %all-to-all-start.1) | async-done | bytes 786464 | tf_op jit(solution)/shard_map/all_to_all | solution.py:21
  128.3 1.2 gather_fusion.1
  131.3 2.0 scatter_custom_fusion.1
  133.5 33.6 %all_to_all.20 = bf16[1,32,12,1024]{3,2,0,1:T(8,128)(2,1)S(1)} all-to-all(bf16[1,32,12,1024]{3,2,0,1:T(8,128)(2,1)S(1)} %bitcast.72), channel_id=1, replica_groups=mesh['dp'=16,'tp'=4,'cp'=8] {'tp','cp'}, dimensions={1} | all-to-all | bytes 1572864 | tf_op jit(solution)/shard_map/all_to_all | solution.py:21
  167.3 1.8 fusion.1
  170.9 1.2 reshape_broadcast_in_dim.7
  172.1 6.0 %all-to-all-start.3 = ((bf16[1,32,12,1024]{3,2,0,1:T(8,128)(2,1)}), bf16[1,32,12,1024]{3,2,0,1:T(8,128)(2,1)S(1)}, u32[]{:S(2)}, u32[]{:S(2)}) async-start(bf16[1,32,12,1024]{3,2,0,1:T(8,128)(2,1)} %bitcast.10), calls=%async_computation.3 | async-start | bytes 2097152 | tf_op jit(solution)/shard_map/all_to_all | solution.py:21
  179.0 2.1 multiply_reduce_fusion
  181.2 22.9 %all-to-all-done.3 = bf16[1,32,12,1024]{3,2,0,1:T(8,128)(2,1)S(1)} async-done(((bf16[1,32,12,1024]{3,2,0,1:T(8,128)(2,1)}), bf16[1,32,12,1024]{3,2,0,1:T(8,128)(2,1)S(1)}, u32[]{:S(2)}, u32[]{:S(2)}) %all-to-all-start.3) | async-done | bytes 786464 | tf_op jit(solution)/shard_map/all_to_all | solution.py:21
  204.2 1.2 gather_fusion.2
  206.1 1.2 reduce_sum.60
  208.3 237.0 %all-reduce.3.cloned.1.call-done = f32[1024,32]{0,1:T(8,128)} async-done(((f32[1024,32]{0,1:T(8,128)}), f32[1024,32]{0,1:T(8,128)}) %all-reduce.3.cloned.1.call-update) | async-done | bytes 131088 | tf_op jit(solution)/shard_map/psum | solution.py:104
  445.3 1.6 copy.73
  (89 shorter events, 14.1 us)
Async XLA Ops:
  7.2 94.5 %copy-start = (bf16[1024,32]{0,1:T(8,128)(2,1)S(1)}, bf16[1024,32]{0,1:T(8,128)(2,1)}, u32[]{:S(2)}) copy-start(bf16[1024,32]{0,1:T(8,128)(2,1)} %param.11) | copy-start | bytes 196612
  13.5 11.8 %copy-start.15 = (bf16[1,384,64]{1,2,0:T(8,128)(2,1)S(1)}, bf16[1,384,64]{1,2,0:T(8,128)(2,1)}, u32[]{:S(2)}) copy-start(bf16[1,384,64]{1,2,0:T(8,128)(2,1)} %param.14) | copy-start | bytes 147460
  14.7 38.2 %copy-start.16 = (bf16[1,64,384]{2,1,0:T(8,128)(2,1)S(1)}, bf16[1,64,384]{2,1,0:T(8,128)(2,1)}, u32[]{:S(2)}) copy-start(bf16[1,64,384]{2,1,0:T(8,128)(2,1)} %param.13) | copy-start | bytes 147460
  14.7 54.8 %copy-start.17 = (bf16[1,64,384]{2,1,0:T(8,128)(2,1)S(1)}, bf16[1,64,384]{2,1,0:T(8,128)(2,1)}, u32[]{:S(2)}) copy-start(bf16[1,64,384]{2,1,0:T(8,128)(2,1)} %param.12) | copy-start | bytes 147460
  14.7 72.7 %all-to-all-start = ((bf16[1,32,12,1024]{3,2,0,1:T(8,128)(2,1)}), bf16[1,32,12,1024]{3,2,0,1:T(8,128)(2,1)S(1)}, u32[]{:S(2)}, u32[]{:S(2)}) async-start(bf16[1,32,12,1024]{3,2,0,1:T(8,128)(2,1)} %bitcast.4), calls=%async_computation | async-start | bytes 2097152 | tf_op jit(solution)/shard_map/all_to_all | solution.py:21
  69.5 18.7 %copy-start.2 = (bf16[1,1024,384]{2,1,0:T(8,128)(2,1)}, bf16[1,1024,384]{2,1,0:T(8,128)(2,1)S(1)}, u32[]{:S(2)}) copy-start(bf16[1,1024,384]{2,1,0:T(8,128)(2,1)S(1)} %all-gather.1) | copy-start | bytes 2359300
  87.4 0.9 copy-start.4
  88.3 0.8 copy-start.12
  88.3 1.6 copy-start.6
  89.1 0.8 copy-start.10
  90.5 10.9 %copy-start.18 = (s32[128,2]{0,1:T(2,128)S(1)}, s32[128,2]{0,1:T(2,128)}, u32[]{:S(2)}) copy-start(s32[128,2]{0,1:T(2,128)} %param.10) | copy-start | bytes 3076
  91.8 9.9 %copy-start.7 = (bf16[128,1024]{1,0:T(8,128)(2,1)S(1)}, bf16[128,1024]{1,0:T(8,128)(2,1)}, u32[]{:S(2)}) copy-start(bf16[128,1024]{1,0:T(8,128)(2,1)} %param.9) | copy-start | bytes 786436
  91.8 36.3 %all-to-all-start.1 = ((bf16[1,32,12,1024]{3,2,0,1:T(8,128)(2,1)}), bf16[1,32,12,1024]{3,2,0,1:T(8,128)(2,1)S(1)}, u32[]{:S(2)}, u32[]{:S(2)}) async-start(bf16[1,32,12,1024]{3,2,0,1:T(8,128)(2,1)} %bitcast.8), calls=%async_computation.1 | async-start | bytes 2097152 | tf_op jit(solution)/shard_map/all_to_all | solution.py:21
  101.9 2.2 copy-start.14
  129.8 1.2 copy-start.8
  129.8 1.5 copy-start.1
  167.1 2.0 copy-start.5
  167.3 1.8 copy-start.11
  167.3 1.8 copy-start.13
  169.1 1.1 copy-start.3
  172.1 6.9 %copy-start.9 = (bf16[128,2,1024]{2,1,0:T(2,128)(2,1)S(1)}, bf16[128,2,1024]{2,1,0:T(2,128)(2,1)}, u32[]{:S(2)}) copy-start(bf16[128,2,1024]{2,1,0:T(2,128)(2,1)} %copy-done.8) | copy-start | bytes 1572868
  172.1 32.0 %all-to-all-start.3 = ((bf16[1,32,12,1024]{3,2,0,1:T(8,128)(2,1)}), bf16[1,32,12,1024]{3,2,0,1:T(8,128)(2,1)S(1)}, u32[]{:S(2)}, u32[]{:S(2)}) async-start(bf16[1,32,12,1024]{3,2,0,1:T(8,128)(2,1)} %bitcast.10), calls=%async_computation.3 | async-start | bytes 2097152 | tf_op jit(solution)/shard_map/all_to_all | solution.py:21
  178.1 267.3 %all-reduce.3.cloned.1.call-start = ((), (), s32[]{:S(2)}) async-start(), calls=%async_computation.4 | async-start | bytes 262144 | tf_op jit(solution)/shard_map/psum | solution.py:104
Sparse Core Ops, SparseCore 0:
  184.5 260.8 all-reduce.2
where the time goes:
time: 454 us
  waiting for transfers between devices  282 us (62%)
  blocking collectives  95.7 us (21%)
  starting transfers between devices  26.3 us (6%)
  local copies, waits for them, and re-layouts  20.4 us (4%)
  between operations  14.4 us (3%)
  matrix products  7.95 us (2%)
  other arithmetic  7.16 us (2%)
    psum x1, waiting for transfers between devices, on_device(): router_grad = lax.psum(router_part, ('dp', 'tp', 'cp'))  237 us
    all_to_all x3, waiting for transfers between devices, trade(): lax.all_to_all(shaped, ('tp', 'cp'), split_axis=1, concat_axis=1, tiled=T...  44.8 us
    all_to_all x1, blocking collectives, trade(): lax.all_to_all(shaped, ('tp', 'cp'), split_axis=1, concat_axis=1, tiled=T...  33.6 us
    all_gather x1, blocking collectives, on_device(): lax.all_gather(down_weight[0], 'dp', axis=1, tiled=True)  27.5 us
    all_to_all x3, starting transfers between devices, trade(): lax.all_to_all(shaped, ('tp', 'cp'), split_axis=1, concat_axis=1, tiled=T...  26.3 us
    all_gather x1, blocking collectives, on_device(): lax.all_gather(gate_weight[0], 'dp', axis=0, tiled=True)  17.9 us
    all_gather x1, blocking collectives, on_device(): lax.all_gather(up_weight[0], 'dp', axis=0, tiled=True)  16.6 us
  transfers between devices with their start and end apart: 4, of which 3 were waited for; matrix products, arithmetic and copies ran while one was open for 3% of the time, Pallas kernels for 0%

commit v1 on v0

--- a/solution.py
+++ b/solution.py
@@ -2,6 +2,22 @@
 import jax.numpy as jnp
 from jax import lax
 from jax.sharding import PartitionSpec as P
+
+
+def gather_around(x, axis, dim):
+    ways, here, step = (lax.axis_size(axis), lax.axis_index(axis), x.shape[dim])
+    lengths = [n * ways if d == dim else n for d, n in enumerate(x.shape)]
+    full = lax.dynamic_update_slice_in_dim(jnp.zeros(lengths, x.dtype), x, here * step, axis=dim)
+    going_up = going_down = x
+    for far in range(1, ways // 2 + 1):
+        going_up = lax.ppermute(going_up, axis, [(d, (d + 1) % ways) for d in range(ways)])
+        full = lax.dynamic_update_slice_in_dim(full, going_up, (here - far) % ways * step, axis=dim)
+        if 2 * far < ways:
+            going_down = lax.ppermute(going_down, axis, [(d, (d - 1) % ways) for d in range(ways)])
+            full = lax.dynamic_update_slice_in_dim(
+                full, going_down, (here + far) % ways * step, axis=dim
+            )
+    return full
 
 
 def route_slots(flat_ids, expert_count):
@@ -56,7 +72,7 @@
     contract = (((1,), (1,)), ((), ()))
     w_gate, w_up, w_down = (
         lax.all_gather(gate_weight[0], "dp", axis=0, tiled=True),
-        lax.all_gather(up_weight[0], "dp", axis=0, tiled=True),
+        gather_around(up_weight[0], "dp", 0),
         lax.all_gather(down_weight[0], "dp", axis=1, tiled=True),
     )
     logits = jnp.dot(tokens, router_weight, preferred_element_type=jnp.float32)

time: 454 us -> 468 us (1.031)
  blocking collectives: 95.7 us -> 72.4 us
  starting transfers between devices: 26.3 us -> 48.1 us
  local copies, waits for them, and re-layouts: 20.4 us -> 31.8 us
    ppermute x0 -> x15, starting transfers between devices: none -> 23.2 us  [the longest x7 13.1 us: gather_around(): lax.ppermute(going_down, axis, [(d, (d - 1) % ways) for d in range(ways)])]
    all_gather x1 -> x0, blocking collectives: 16.6 us -> none  [on_device(): lax.all_gather(up_weight[0], 'dp', axis=0, tiled=True)]
    dynamic_update_slice x0 -> x16, local copies, waits for them, and re-layouts: none -> 10.7 us  [the longest x8 5.79 us: gather_around(): lax.dynamic_update_slice_in_dim(full, going_up, (here - far) % ways * ste...]
  transfers between devices with their start and end apart: 4 -> 19, of which waited for: 3 -> 7; matrix products, arithmetic and copies ran while one was open for 3% -> 7% of each run, Pallas kernels for 0% -> 0%
where the time goes in v1:
time: 468 us
  waiting for transfers between devices  285 us (61%)
  blocking collectives  72.4 us (15%)
  starting transfers between devices  48.1 us (10%)
  local copies, waits for them, and re-layouts  31.8 us (7%)
  between operations  14.5 us (3%)
  matrix products  9 us (2%)
  other arithmetic  7.13 us (2%)
    psum x1, waiting for transfers between devices, on_device(): router_grad = lax.psum(router_part, ('dp', 'tp', 'cp'))  240 us
    all_to_all x3, waiting for transfers between devices, trade(): lax.all_to_all(shaped, ('tp', 'cp'), split_axis=1, concat_axis=1, tiled=T...  40.8 us
    all_to_all x1, blocking collectives, trade(): lax.all_to_all(shaped, ('tp', 'cp'), split_axis=1, concat_axis=1, tiled=T...  30.5 us
    all_gather x1, blocking collectives, on_device(): lax.all_gather(down_weight[0], 'dp', axis=1, tiled=True)  25.2 us
    all_to_all x3, starting transfers between devices, trade(): lax.all_to_all(shaped, ('tp', 'cp'), split_axis=1, concat_axis=1, tiled=T...  24.7 us
    all_gather x1, blocking collectives, on_device(): lax.all_gather(gate_weight[0], 'dp', axis=0, tiled=True)  16.6 us
    ppermute x7, starting transfers between devices, gather_around(): lax.ppermute(going_down, axis, [(d, (d - 1) % ways) for d in range(ways)])  13.1 us
    ppermute x8, starting transfers between devices, gather_around(): lax.ppermute(going_up, axis, [(d, (d + 1) % ways) for d in range(ways)])  10 us
  transfers between devices with their start and end apart: 19, of which 7 were waited for; matrix products, arithmetic and copies ran while one was open for 7% of the time, Pallas kernels for 0%

profile of v1, /device:TPU:1, one launch (start us, length us, event | category | flops | bytes accessed | tf_op | source)
XLA Modules:
  0.0 467.5 jit_solution(3872345055317075802)
XLA Ops:
  7.2 3.5 collective-permute-start
  10.7 3.4 collective-permute-start.1
  18.5 1.9 scatter_custom_fusion
  21.6 6.4 %all-to-all-start = ((bf16[1,32,12,1024]{3,2,0,1:T(8,128)(2,1)}), bf16[1,32,12,1024]{3,2,0,1:T(8,128)(2,1)S(1)}, u32[]{:S(2)}, u32[]{:S(2)}) async-start(bf16[1,32,12,1024]{3,2,0,1:T(8,128)(2,1)} %bitcast.4), calls=%async_computation | async-start | bytes 2097152 | tf_op jit(solution)/shard_map/all_to_all | solution.py:37
  28.0 25.2 %all-gather.1 = bf16[1,384,1024]{1,2,0:T(8,128)(2,1)S(1)} all-gather(bf16[1,384,64]{1,2,0:T(8,128)(2,1)S(1)} %copy-done.14), channel_id=3, replica_groups=mesh['dp'=16,'tp'=4,'cp'=8] {'dp'}, dimensions={2}, use_global_device_ids=true | all-gather | bytes 835584 | tf_op jit(solution)/shard_map/all_gather | solution.py:76
  53.2 16.6 %all-gather = bf16[1,1024,384]{2,1,0:T(8,128)(2,1)S(1)} all-gather(bf16[1,64,384]{2,1,0:T(8,128)(2,1)S(1)} %copy-done.15), channel_id=2, replica_groups=mesh['dp'=16,'tp'=4,'cp'=8] {'dp'}, dimensions={1}, use_global_device_ids=true | all-gather | bytes 835584 | tf_op jit(solution)/shard_map/all_gather | solution.py:74
  74.9 1.7 collective-permute-start.4
  77.9 2.3 collective-permute-start.6
  84.0 2.1 collective-permute-start.9
  87.5 3.3 collective-permute-start.11
  92.0 3.5 collective-permute-start.13
  98.0 2.9 collective-permute-done.14
  101.8 1.7 fusion.30
  106.4 9.8 %all-to-all-start.1 = ((bf16[1,32,12,1024]{3,2,0,1:T(8,128)(2,1)}), bf16[1,32,12,1024]{3,2,0,1:T(8,128)(2,1)S(1)}, u32[]{:S(2)}, u32[]{:S(2)}) async-start(bf16[1,32,12,1024]{3,2,0,1:T(8,128)(2,1)} %bitcast.8), calls=%async_computation.1 | async-start | bytes 2097152 | tf_op jit(solution)/shard_map/all_to_all | solution.py:37
  116.6 2.0 gather_fusion
  119.2 1.7 mul.162
  120.9 18.6 %all-to-all-done.1 = bf16[1,32,12,1024]{3,2,0,1:T(8,128)(2,1)S(1)} async-done(((bf16[1,32,12,1024]{3,2,0,1:T(8,128)(2,1)}), bf16[1,32,12,1024]{3,2,0,1:T(8,128)(2,1)S(1)}, u32[]{:S(2)}, u32[]{:S(2)}) %all-to-all-start.1) | async-done | bytes 786464 | tf_op jit(solution)/shard_map/all_to_all | solution.py:37
  142.7 2.0 scatter_custom_fusion.1
  144.9 30.5 %all_to_all.20 = bf16[1,32,12,1024]{3,2,0,1:T(8,128)(2,1)S(1)} all-to-all(bf16[1,32,12,1024]{3,2,0,1:T(8,128)(2,1)S(1)} %bitcast.71), channel_id=1, replica_groups=mesh['dp'=16,'tp'=4,'cp'=8] {'tp','cp'}, dimensions={1} | all-to-all | bytes 1572864 | tf_op jit(solution)/shard_map/all_to_all | solution.py:37
  177.8 1.8 add_convert_fusion
  180.7 8.5 %all-to-all-start.3 = ((bf16[1,32,12,1024]{3,2,0,1:T(8,128)(2,1)}), bf16[1,32,12,1024]{3,2,0,1:T(8,128)(2,1)S(1)}, u32[]{:S(2)}, u32[]{:S(2)}) async-start(bf16[1,32,12,1024]{3,2,0,1:T(8,128)(2,1)} %bitcast.10), calls=%async_computation.3 | async-start | bytes 2097152 | tf_op jit(solution)/shard_map/all_to_all | solution.py:37
  190.4 2.1 multiply_reduce_fusion
  192.5 22.2 %all-to-all-done.3 = bf16[1,32,12,1024]{3,2,0,1:T(8,128)(2,1)S(1)} async-done(((bf16[1,32,12,1024]{3,2,0,1:T(8,128)(2,1)}), bf16[1,32,12,1024]{3,2,0,1:T(8,128)(2,1)S(1)}, u32[]{:S(2)}, u32[]{:S(2)}) %all-to-all-start.3) | async-done | bytes 786464 | tf_op jit(solution)/shard_map/all_to_all | solution.py:37
  219.0 240.1 %all-reduce.3.cloned.1.call-done = f32[1024,32]{0,1:T(8,128)} async-done(((f32[1024,32]{0,1:T(8,128)}), f32[1024,32]{0,1:T(8,128)}) %all-reduce.3.cloned.1.call-update) | async-done | bytes 131088 | tf_op jit(solution)/shard_map/psum | solution.py:120
  (133 shorter events, 39.3 us)
Async XLA Ops:
  7.2 109.3 %copy-start = (bf16[1024,32]{0,1:T(8,128)(2,1)S(1)}, bf16[1024,32]{0,1:T(8,128)(2,1)}, u32[]{:S(2)}) copy-start(bf16[1024,32]{0,1:T(8,128)(2,1)} %param.11) | copy-start | bytes 196612
  7.2 64.3 %collective-permute-start = (bf16[64,384]{1,0:T(8,128)(2,1)}, bf16[64,384]{1,0:T(8,128)(2,1)}, u32[]{:S(2)}, u32[]{:S(2)}) collective-permute-start(bf16[64,384]{1,0:T(8,128)(2,1)} %bitcast.73), channel_id=1, source_target_pairs={{0,32},{32,64},{64,96},{96,128},{128,160},{160,192},{192,224},{224... | collective-permute-start | bytes 147464 | tf_op jit(solution)/shard_map/ppermute | solution.py:13
  10.7 62.2 %collective-permute-start.1 = (bf16[64,384]{1,0:T(8,128)(2,1)}, bf16[64,384]{1,0:T(8,128)(2,1)S(1)}, u32[]{:S(2)}, u32[]{:S(2)}) collective-permute-start(bf16[64,384]{1,0:T(8,128)(2,1)} %bitcast.74), channel_id=1, source_target_pairs={{0,480},{32,0},{64,32},{96,64},{128,96},{160,128},{192,160},{224,1... | collective-permute-start | bytes 147464 | tf_op jit(solution)/shard_map/ppermute | solution.py:16
  21.6 31.6 %copy-start.15 = (bf16[1,64,384]{2,1,0:T(8,128)(2,1)S(1)}, bf16[1,64,384]{2,1,0:T(8,128)(2,1)}, u32[]{:S(2)}) copy-start(bf16[1,64,384]{2,1,0:T(8,128)(2,1)} %param.12) | copy-start | bytes 147460
  21.6 80.0 %all-to-all-start = ((bf16[1,32,12,1024]{3,2,0,1:T(8,128)(2,1)}), bf16[1,32,12,1024]{3,2,0,1:T(8,128)(2,1)S(1)}, u32[]{:S(2)}, u32[]{:S(2)}) async-start(bf16[1,32,12,1024]{3,2,0,1:T(8,128)(2,1)} %bitcast.4), calls=%async_computation | async-start | bytes 2097152 | tf_op jit(solution)/shard_map/all_to_all | solution.py:37
  28.0 42.9 %copy-start.16 = (bf16[1,64,384]{2,1,0:T(8,128)(2,1)S(1)}, bf16[1,64,384]{2,1,0:T(8,128)(2,1)}, u32[]{:S(2)}) copy-start(bf16[1,64,384]{2,1,0:T(8,128)(2,1)} %param.13) | copy-start | bytes 147460
  53.2 50.9 %copy-start.2 = (bf16[1,384,1024]{1,2,0:T(8,128)(2,1)}, bf16[1,384,1024]{1,2,0:T(8,128)(2,1)S(1)}, u32[]{:S(2)}) copy-start(bf16[1,384,1024]{1,2,0:T(8,128)(2,1)S(1)} %all-gather.1) | copy-start | bytes 2359300
  69.8 33.7 %copy-start.4 = (bf16[1,1024,384]{2,1,0:T(8,128)(2,1)}, bf16[1,1024,384]{2,1,0:T(8,128)(2,1)S(1)}, u32[]{:S(2)}) copy-start(bf16[1,1024,384]{2,1,0:T(8,128)(2,1)S(1)} %all-gather) | copy-start | bytes 2359300
  71.4 3.5 collective-permute-start.2
  72.9 3.8 collective-permute-start.3
  74.9 3.0 collective-permute-start.4
  76.7 3.8 collective-permute-start.5
  77.9 4.7 collective-permute-start.6
  80.5 3.5 collective-permute-start.7
  82.6 4.7 %collective-permute-start.8 = (bf16[64,384]{1,0:T(8,128)(2,1)S(1)}, bf16[64,384]{1,0:T(8,128)(2,1)S(1)}, u32[]{:S(2)}, u32[]{:S(2)}) collective-permute-start(bf16[64,384]{1,0:T(8,128)(2,1)S(1)} %collective-permute-done.6), channel_id=1, source_target_pairs={{0,32},{32,64},{64,96},{96,128},{128,160},{160,192},{192,224},{224... | collective-permute-start | bytes 147464 | tf_op jit(solution)/shard_map/ppermute | solution.py:13
  84.0 3.5 collective-permute-start.9
  87.3 4.7 %collective-permute-start.10 = (bf16[64,384]{1,0:T(8,128)(2,1)S(1)}, bf16[64,384]{1,0:T(8,128)(2,1)S(1)}, u32[]{:S(2)}, u32[]{:S(2)}) collective-permute-start(bf16[64,384]{1,0:T(8,128)(2,1)S(1)} %collective-permute-done.8), channel_id=1, source_target_pairs={{0,32},{32,64},{64,96},{96,128},{128,160},{160,192},{192,224},{224... | collective-permute-start | bytes 147464 | tf_op jit(solution)/shard_map/ppermute | solution.py:13
  87.5 4.5 collective-permute-start.11
  92.0 4.8 %collective-permute-start.12 = (bf16[64,384]{1,0:T(8,128)(2,1)S(1)}, bf16[64,384]{1,0:T(8,128)(2,1)S(1)}, u32[]{:S(2)}, u32[]{:S(2)}) collective-permute-start(bf16[64,384]{1,0:T(8,128)(2,1)S(1)} %collective-permute-done.10), channel_id=1, source_target_pairs={{0,32},{32,64},{64,96},{96,128},{128,160},{160,192},{192,224},{224... | collective-permute-start | bytes 147464 | tf_op jit(solution)/shard_map/ppermute | solution.py:13
  92.0 5.4 %collective-permute-start.13 = (bf16[64,384]{1,0:T(8,128)(2,1)S(1)}, bf16[64,384]{1,0:T(8,128)(2,1)S(1)}, u32[]{:S(2)}, u32[]{:S(2)}) collective-permute-start(bf16[64,384]{1,0:T(8,128)(2,1)S(1)} %collective-permute-done.11), channel_id=1, source_target_pairs={{0,480},{32,0},{64,32},{96,64},{128,96},{160,128},{192,160},{224,1... | collective-permute-start | bytes 147464 | tf_op jit(solution)/shard_map/ppermute | solution.py:16
  96.8 4.2 collective-permute-start.14
  106.4 33.1 %all-to-all-start.1 = ((bf16[1,32,12,1024]{3,2,0,1:T(8,128)(2,1)}), bf16[1,32,12,1024]{3,2,0,1:T(8,128)(2,1)S(1)}, u32[]{:S(2)}, u32[]{:S(2)}) async-start(bf16[1,32,12,1024]{3,2,0,1:T(8,128)(2,1)} %bitcast.8), calls=%async_computation.1 | async-start | bytes 2097152 | tf_op jit(solution)/shard_map/all_to_all | solution.py:37
  180.7 34.0 %all-to-all-start.3 = ((bf16[1,32,12,1024]{3,2,0,1:T(8,128)(2,1)}), bf16[1,32,12,1024]{3,2,0,1:T(8,128)(2,1)S(1)}, u32[]{:S(2)}, u32[]{:S(2)}) async-start(bf16[1,32,12,1024]{3,2,0,1:T(8,128)(2,1)} %bitcast.10), calls=%async_computation.3 | async-start | bytes 2097152 | tf_op jit(solution)/shard_map/all_to_all | solution.py:37
  189.2 269.9 %all-reduce.3.cloned.1.call-start = ((), (), s32[]{:S(2)}) async-start(), calls=%async_computation.4 | async-start | bytes 262144 | tf_op jit(solution)/shard_map/psum | solution.py:120
  (13 other events, 79.6 us)
Sparse Core Ops, SparseCore 0:
  195.6 263.4 all-reduce.2
